TPU v7x, 32 devices: a whole 2x2x4 slice. The times are simulated.
32 devices in a mesh: member: 2 (over core), grid: 16 (over z, y, x).
Axes of the slice: x: 2, y: 2, z: 4, core: 2. Of those that a mesh axis runs over, the one named last changes fastest.
Arguments:
- latent: bfloat16 [4, 32768, 512], P('member', 'grid'), may hold values from -80 to 80
- block_pick: int32 [16, 16], P('grid'), may hold values from 0 to 15
- obs_weight: bfloat16 [16, 16, 128, 128], P('grid'), may hold values from 0.0099487305 to 1
- obs_value: float32 [16, 16, 128, 128], P('grid'), may hold values from -6 to 6
- obs_count: int32 [16, 16], P('grid'), may hold values from 0 to 128, as said below
- w_in: bfloat16 [512, 512], replicated, may hold values from -0.25 to 0.25
- b_in: float32 [512], replicated, may hold values from -3 to 3
- w_out: bfloat16 [512, 128], replicated, may hold values from -0.25 to 0.25
- b_out: float32 [128], replicated, may hold values from -3 to 3
Outputs:
- latent_grad: float32 [4, 32768, 512], P('member', 'grid')
- loss_value: float32 [], replicated
Inputs may be any that keep to these rules, and one draw needn't show every extreme that they name: Entry [d, j] counts the live observations of those slots; the live ones are the first slots, k < obs_count[d, j].
All inputs are finite; a program needn't handle non-finite values.
Results may differ from a plain program's by a relative error of at most 0.0041.
Values may be sent and summed in bfloat16 or wider, within the bound.
A program may use at most 128 MiB of HBM per device.

v0:
```python
import jax
import jax.numpy as jnp
from jax import lax
from jax.sharding import PartitionSpec as P

SOFTEN = 0.1


def smooth_abs(value):
    return jnp.sqrt(value * value + SOFTEN * SOFTEN)


def silu_slope(pre_act):
    sigmoid_value = jax.nn.sigmoid(pre_act)
    return sigmoid_value * (1.0 + pre_act * (1.0 - sigmoid_value))


def per_device(latent, block_pick, obs_weight, obs_value, obs_count, w_in, b_in, w_out, b_out):
    members_here, points, feature_width = latent.shape
    peer_count = lax.axis_size("grid")
    slot_count = obs_weight.shape[2]
    block_size = obs_weight.shape[3]
    channels = obs_value.shape[3]
    members_all = members_here * lax.axis_size("member")
    block_count = points // block_size
    local_blocks = latent.reshape(members_here, block_count, block_size, feature_width)
    picked_ids = block_pick[0]
    block_onehot = (
        picked_ids[:, None] == jnp.arange(block_count, dtype=jnp.int32)[None, :]
    ).astype(jnp.bfloat16)
    weight_sum = jnp.sum(obs_weight[0], axis=2, keepdims=True, dtype=jnp.float32)
    norm_weight = (obs_weight[0] / weight_sum).astype(jnp.bfloat16)
    picked = local_blocks[:, picked_ids]
    interp = jnp.einsum(
        "jkp,mjpc->mjkc",
        norm_weight,
        lax.all_to_all(picked, "grid", split_axis=1, concat_axis=1, tiled=True),
        preferred_element_type=jnp.float32,
    ).astype(jnp.bfloat16)
    flat_rows = interp.reshape(members_here * peer_count * slot_count, feature_width)
    pre_act = jnp.dot(flat_rows, w_in, preferred_element_type=jnp.float32) + b_in
    hidden = jax.nn.silu(pre_act).astype(jnp.bfloat16)
    predicted = jnp.dot(hidden, w_out, preferred_element_type=jnp.float32) + b_out
    predicted = predicted.reshape(members_here, peer_count, slot_count, channels)
    all_members = lax.all_gather(predicted, "member", axis=0, tiled=True)
    target = obs_value[0]
    live_mask = (jnp.arange(slot_count, dtype=jnp.int32)[None, :] < obs_count[0][:, None]).astype(
        jnp.float32
    )
    obs_diff = predicted - target[None]
    pair_diff = predicted[:, None] - all_members[None]
    per_obs = smooth_abs(obs_diff) / members_all - jnp.sum(smooth_abs(pair_diff), axis=1) / (
        2.0 * members_all * (members_all - 1)
    )
    loss_part = jnp.sum(per_obs * live_mask[None, :, :, None])
    live_count = jnp.sum(live_mask)
    live_total = lax.psum(live_count, "grid")
    loss_total = lax.psum(loss_part, ("member", "grid"))
    loss_value = loss_total / (channels * live_total)
    grad_scale = peer_count * peer_count * slot_count / live_total
    slope_obs = obs_diff / smooth_abs(obs_diff)
    slope_pair = jnp.sum(pair_diff / smooth_abs(pair_diff), axis=1)
    grad_pred = (
        grad_scale
        * live_mask[None, :, :, None]
        * (slope_obs / members_all - slope_pair / (members_all * (members_all - 1.0)))
    ).astype(jnp.bfloat16)
    grad_hidden = jnp.einsum(
        "rv,hv->rh", grad_pred.reshape(-1, channels), w_out, preferred_element_type=jnp.float32
    )
    grad_act = (grad_hidden * silu_slope(pre_act)).astype(jnp.bfloat16)
    grad_interp = jnp.einsum(
        "rh,ch->rc", grad_act, w_in, preferred_element_type=jnp.float32
    ).astype(jnp.bfloat16)
    grad_interp = grad_interp.reshape(members_here, peer_count, slot_count, feature_width)
    contribution = jnp.einsum(
        "jkp,mjkc->mjpc", norm_weight, grad_interp, preferred_element_type=jnp.float32
    ).astype(jnp.bfloat16)
    returned = lax.all_to_all(contribution, "grid", split_axis=1, concat_axis=1, tiled=True)
    summed = jnp.einsum("mdpc,db->mbpc", returned, block_onehot, preferred_element_type=jnp.float32)
    latent_grad = summed.reshape(members_here, points, feature_width)
    return (latent_grad, loss_value)


def solution(mesh):
    in_specs = (
        P("member", "grid", None),
        P("grid", None),
        P("grid", None, None, None),
        P("grid", None, None, None),
        P("grid", None),
        P(),
        P(),
        P(),
        P(),
    )
    out_specs = (P("member", "grid", None), P())
    return jax.shard_map(
        per_device, mesh=mesh, in_specs=in_specs, out_specs=out_specs, check_vma=False
    )
```

profile of v0, /device:TPU:25, one launch (start us, length us, event | category | flops | bytes accessed | tf_op | source)
XLA Modules:
  0.0 329.2 jit_solution(2911062721672756190)
XLA Ops:
  7.2 0.0 copy-start
  7.2 0.7 fusion.26
  7.9 5.0 %gather_fusion = bf16[16,2,128,512]{3,2,1,0:T(8,128)(2,1)} fusion(bf16[2,16,128,512]{3,2,1,0:T(8,128)(2,1)} %bitcast.72, s32[1024]{0:T(1024)S(1)} %pad_clamp_fusion), kind=kCustom, calls=%fused_computation | custom fusion | bytes 8388672 | tf_op jit(solution)/shard_map/gather | solution.py:33
  12.9 0.0 copy-start.4
  12.9 6.6 %all-to-all-start = ((bf16[2,16,128,512]{3,2,0,1:T(8,128)(2,1)}), bf16[2,16,128,512]{3,2,0,1:T(8,128)(2,1)}, u32[]{:S(2)}, u32[]{:S(2)}) async-start(bf16[2,16,128,512]{3,2,0,1:T(8,128)(2,1)} %bitcast.70), calls=%async_computation | async-start | bytes 8388608 | tf_op jit(solution)/shard_map/all_to_all | solution.py:37
  19.5 0.0 all-gather.2.cloned.1.call-start
  19.5 0.0 copy-done.4
  19.5 0.2 convert_reduce_fusion
  19.8 87.2 %all-to-all-done = bf16[2,16,128,512]{3,2,0,1:T(8,128)(2,1)} async-done(((bf16[2,16,128,512]{3,2,0,1:T(8,128)(2,1)}), bf16[2,16,128,512]{3,2,0,1:T(8,128)(2,1)}, u32[]{:S(2)}, u32[]{:S(2)}) %all-to-all-start) | async-done | bytes 4194336 | tf_op jit(solution)/shard_map/all_to_all | solution.py:37
  107.0 3.5 %convert_bitcast_fusion.1 = bf16[2,16,128,512]{3,2,0,1:T(8,128)(2,1)S(1)} fusion(bf16[2,16,128,512]{3,2,0,1:T(8,128)(2,1)} %all-to-all-done, bf16[1,16,128,128]{3,2,1,0:T(8,128)(2,1)S(1)} %copy-done.4, f32[16,128]{1,0:T(8,128)S(1)} %convert_reduce_fusion), kind=kOutput, calls=%fused_computation.17 | convolution fusion | flops 539754496 | bytes 8921088 | tf_op jit(solution)/shard_map/jkp,mjpc->mjkc/dot_general | solution.py:34
  110.5 0.4 copy.18
  110.9 0.0 copy-done
  110.9 0.0 copy-start.8
  111.0 0.0 copy-start.9
  111.0 0.0 copy-start.10
  111.0 2.4 fusion.31
  113.4 0.0 copy-done.8
  113.4 0.0 copy-done.9
  113.4 0.0 copy-done.10
  113.4 0.0 copy-start.3
  113.5 0.0 copy-start.6
  113.5 4.1 %convolution_add_fusion = f32[4096,128]{1,0:T(8,128)} fusion(bf16[512,128]{1,0:T(8,128)(2,1)S(1)} %copy-done.8, f32[4096,512]{1,0:T(8,128)S(1)} %fusion.31, f32[512]{0:T(512)S(1)} %copy-done.9, f32[128]{0:T(128)S(1)} %copy-done.10), kind=kOutput, calls=%fused_computation.11 | convolution fusion | flops 549978112 | bytes 10619392 | tf_op jit(solution)/shard_map/dot_general | solution.py:43
  117.5 0.0 copy-done.3
  117.5 0.0 all-gather.2.cloned.1.call-update
  117.6 0.0 copy-done.6
  117.6 0.7 fusion.25
  118.2 31.0 %psum.14 = f32[]{:T(128)} all-reduce(f32[]{:T(128)} %fusion.25), channel_id=1, replica_groups=mesh['member'=2,'grid'=16] {'grid'}, use_global_device_ids=true, to_apply=%region_1.2 | all-reduce | flops 1 | bytes 8 | tf_op jit(solution)/shard_map/psum | solution.py:57
  150.0 0.1 fusion.21
  150.0 0.1 fusion.20
  150.1 0.0 all-gather.2.cloned.1.call-done
  150.1 7.3 %fusion.2 = (f32[2,16,128,128]{3,2,1,0:T(8,128)S(1)}, f32[2,16,128,128]{3,2,1,0:T(8,128)S(1)}) fusion(f32[4,16,128,128]{3,2,1,0:T(8,128)} %all-gather.2.cloned.1.call-done, f32[2,16,128,128]{3,2,1,0:T(8,128)} %bitcast.68), kind=kLoop, calls=%fused_computation.5 | loop fusion | flops 11534336 | bytes 10485760 | tf_op jit(solution)/shard_map/reduce_sum | solution.py:52
  157.4 0.0 copy-start.2
  157.4 0.0 copy-start.5
  157.4 0.7 broadcast_multiply_fusion
  158.2 0.8 copy-done.2
  159.0 0.3 copy-done.5
  159.3 2.5 fusion.14
  161.8 8.6 %convolution_convert_fusion = bf16[4096,512]{1,0:T(8,128)(2,1)} fusion(bf16[512,512]{1,0:T(8,128)(2,1)S(1)} %copy-done, f32[4096,512]{1,0:T(8,128)} %copy-done.3, bf16[4096,128]{1,0:T(8,128)(2,1)S(1)} %get-tuple-element.5, bf16[512,128]{1,0:T(8,128)(2,1)S(1)} %copy-done.8, f32[512]{0:T(512)S(1)} %copy-done.9), kind=kOutput, calls=%fused_computation.10 | convolution fusion | flops 2707423232 | bytes 14288896 | tf_op jit(solution)/shard_map/rh,ch->rc/dot_general | solution.py:72
  170.4 5.9 %convert_bitcast_fusion = bf16[2,16,128,512]{2,3,0,1:T(8,128)(2,1)} fusion(bf16[2,16,128,512]{3,2,1,0:T(8,128)(2,1)} %bitcast.80, bf16[1,16,128,128]{3,2,1,0:T(8,128)(2,1)S(1)} %copy-done.4, f32[16,128]{1,0:T(8,128)S(1)} %convert_reduce_fusion), kind=kOutput, calls=%fused_computation.16 | convolution fusion | flops 539754496 | bytes 8921088 | tf_op jit(solution)/shard_map/jkp,mjkc->mjpc/dot_general | solution.py:76
  176.3 6.4 %copy.20 = bf16[2,16,128,512]{3,2,0,1:T(8,128)(2,1)} copy(bf16[2,16,128,512]{2,3,0,1:T(8,128)(2,1)} %convert_bitcast_fusion) | data formatting | bytes 8388608 | tf_op jit(solution)/shard_map/convert_element_type | solution.py:78
  182.7 0.0 copy-start.7
  182.7 12.7 %all-to-all-start.1 = ((bf16[2,16,128,512]{3,2,0,1:T(8,128)(2,1)}), bf16[2,16,128,512]{3,2,0,1:T(8,128)(2,1)}, u32[]{:S(2)}, u32[]{:S(2)}) async-start(bf16[2,16,128,512]{3,2,0,1:T(8,128)(2,1)} %copy.20), calls=%async_computation.1 | async-start | bytes 8388608 | tf_op jit(solution)/shard_map/all_to_all | solution.py:79
  196.0 111.5 %psum.15 = f32[]{:T(128)} all-reduce(f32[]{:T(128)} %get-tuple-element.4), channel_id=1, replica_groups=mesh['member'=2,'grid'=16] {'member','grid'}, use_global_device_ids=true, to_apply=%region_6.7 | all-reduce | flops 1 | bytes 8 | tf_op jit(solution)/shard_map/psum | solution.py:58
  308.2 0.0 all-to-all-done.1
  308.2 0.0 copy-done.7
  308.2 4.7 %fusion.8 = f32[2,16,128,512]{3,1,2,0:T(8,128)S(1)} fusion(bf16[2,16,128,512]{3,2,0,1:T(8,128)(2,1)} %all-to-all-done.1, s32[16]{0:T(128)S(1)} %bitcast.79), kind=kOutput, calls=%fused_computation.18 | convolution fusion | flops 67109120 | bytes 12582976 | tf_op jit(solution)/shard_map/mdpc,db->mbpc/dot_general | solution.py:80
  312.9 0.0 copy-start.1
  313.0 8.3 %copy.22 = f32[2,16,128,512]{3,2,1,0:T(8,128)} copy(f32[2,16,128,512]{3,1,2,0:T(8,128)S(1)} %fusion.8) | data formatting | bytes 16777216 | tf_op jit(solution)/shard_map/mdpc,db->mbpc/transpose | solution.py:80
  321.2 0.0 copy-done.1
  (3 shorter events, 0.0 us)
Async XLA Ops:
  7.2 103.8 %copy-start = (bf16[512,512]{1,0:T(8,128)(2,1)S(1)}, bf16[512,512]{1,0:T(8,128)(2,1)}, u32[]{:S(2)}) copy-start(bf16[512,512]{1,0:T(8,128)(2,1)} %param.14) | copy-start | bytes 1572868
  12.9 6.6 %copy-start.4 = (bf16[1,16,128,128]{3,2,1,0:T(8,128)(2,1)S(1)}, bf16[1,16,128,128]{3,2,1,0:T(8,128)(2,1)}, u32[]{:S(2)}) copy-start(bf16[1,16,128,128]{3,2,1,0:T(8,128)(2,1)} %param.11) | copy-start | bytes 1572868
  12.9 94.1 %all-to-all-start = ((bf16[2,16,128,512]{3,2,0,1:T(8,128)(2,1)}), bf16[2,16,128,512]{3,2,0,1:T(8,128)(2,1)}, u32[]{:S(2)}, u32[]{:S(2)}) async-start(bf16[2,16,128,512]{3,2,0,1:T(8,128)(2,1)} %bitcast.70), calls=%async_computation | async-start | bytes 8388608 | tf_op jit(solution)/shard_map/all_to_all | solution.py:37
  19.5 130.6 %all-gather.2.cloned.1.call-start = ((), (), s32[]{:S(2)}) async-start(), calls=%async_computation.2 | async-start | bytes 6291456 | tf_op jit(solution)/shard_map/all_gather | solution.py:45
  110.9 2.5 copy-start.8
  111.0 2.5 copy-start.9
  111.0 2.5 copy-start.10
  113.4 4.1 %copy-start.3 = (f32[4096,512]{1,0:T(8,128)}, f32[4096,512]{1,0:T(8,128)S(1)}, u32[]{:S(2)}) copy-start(f32[4096,512]{1,0:T(8,128)S(1)} %fusion.31) | copy-start | bytes 25165828
  113.5 4.1 %copy-start.6 = (s32[1,16]{1,0:T(1,128)S(1)}, s32[1,16]{1,0:T(1,128)}, u32[]{:S(2)}) copy-start(s32[1,16]{1,0:T(1,128)} %param.13) | copy-start | bytes 196
  157.4 1.6 copy-start.2
  157.4 1.8 copy-start.5
  182.7 125.5 %copy-start.7 = (s32[1,16]{1,0:T(1,128)S(1)}, s32[1,16]{1,0:T(1,128)}, u32[]{:S(2)}) copy-start(s32[1,16]{1,0:T(1,128)} %param.10) | copy-start | bytes 196
  182.7 125.5 %all-to-all-start.1 = ((bf16[2,16,128,512]{3,2,0,1:T(8,128)(2,1)}), bf16[2,16,128,512]{3,2,0,1:T(8,128)(2,1)}, u32[]{:S(2)}, u32[]{:S(2)}) async-start(bf16[2,16,128,512]{3,2,0,1:T(8,128)(2,1)} %copy.20), calls=%async_computation.1 | async-start | bytes 8388608 | tf_op jit(solution)/shard_map/all_to_all | solution.py:79
  312.9 8.3 %copy-start.1 = (bf16[512,512]{1,0:T(8,128)(2,1)S(1)}, bf16[512,512]{1,0:T(8,128)(2,1)}, u32[]{:S(2)}) copy-start(bf16[512,512]{1,0:T(8,128)(2,1)} %param.14) | copy-start | bytes 1572868
Sparse Core Ops, SparseCore 0:
  117.7 21.3 all-gather.1
where the time goes:
time: 333 us; the launch traced here: 329 us
  blocking collectives  143 us (43%)
  waiting for transfers between devices  87.3 us (26%)
  matrix products  29.2 us (9%)
  local copies, waits for them, and re-layouts  21.3 us (6%)
  starting transfers between devices  19.3 us (6%)
  between operations  17.4 us (5%)
  other arithmetic  12.3 us (4%)
    psum x1, blocking collectives, per_device(): loss_total = lax.psum(loss_part, ('member', 'grid'))  111 us
    all_to_all x1, waiting for transfers between devices, per_device(): lax.all_to_all(picked, 'grid', split_axis=1, concat_axis=1, tiled=True)  87.2 us
    psum x1, blocking collectives, per_device(): live_total = lax.psum(live_count, 'grid')  31 us
    all_to_all x1, starting transfers between devices, per_device(): lax.all_to_all(contribution, 'grid', split_axis=1, concat_axis=1, tiled=T...  12.7 us
    dot_general x1, matrix products, per_device(): jnp.einsum('rh,ch->rc', grad_act, w_in, preferred_element_type=jnp.float32)  8.64 us
    transpose x1, local copies, waits for them, and re-layouts, per_device(): jnp.einsum('mdpc,db->mbpc', returned, block_onehot, preferred_element_typ...  8.25 us
    reduce_sum x1, other arithmetic, per_device(): jnp.sum(smooth_abs(pair_diff), axis=1)  7.3 us
  transfers between devices with their start and end apart: 3, of which 1 were waited for; matrix products, arithmetic and copies ran while one was open for 0% of the time, Pallas kernels for 0%

commit v1 on v0

--- a/solution.py
+++ b/solution.py
@@ -28,14 +28,15 @@
     block_onehot = (
         picked_ids[:, None] == jnp.arange(block_count, dtype=jnp.int32)[None, :]
     ).astype(jnp.bfloat16)
-    weight_sum = jnp.sum(obs_weight[0], axis=2, keepdims=True, dtype=jnp.float32)
-    norm_weight = (obs_weight[0] / weight_sum).astype(jnp.bfloat16)
+    weights_here = lax.all_to_all(obs_weight[0], "grid", split_axis=0, concat_axis=0, tiled=True)
+    target = lax.all_to_all(obs_value[0], "grid", split_axis=0, concat_axis=0, tiled=True)
+    counts = lax.all_gather(obs_count[0], "grid", axis=0)
+    counts_here = lax.dynamic_index_in_dim(counts, lax.axis_index("grid"), axis=1, keepdims=False)
+    weight_sum = jnp.sum(weights_here, axis=2, keepdims=True, dtype=jnp.float32)
+    norm_weight = (weights_here / weight_sum).astype(jnp.bfloat16)
     picked = local_blocks[:, picked_ids]
     interp = jnp.einsum(
-        "jkp,mjpc->mjkc",
-        norm_weight,
-        lax.all_to_all(picked, "grid", split_axis=1, concat_axis=1, tiled=True),
-        preferred_element_type=jnp.float32,
+        "jkp,mjpc->mjkc", norm_weight, picked, preferred_element_type=jnp.float32
     ).astype(jnp.bfloat16)
     flat_rows = interp.reshape(members_here * peer_count * slot_count, feature_width)
     pre_act = jnp.dot(flat_rows, w_in, preferred_element_type=jnp.float32) + b_in
@@ -43,8 +44,7 @@
     predicted = jnp.dot(hidden, w_out, preferred_element_type=jnp.float32) + b_out
     predicted = predicted.reshape(members_here, peer_count, slot_count, channels)
     all_members = lax.all_gather(predicted, "member", axis=0, tiled=True)
-    target = obs_value[0]
-    live_mask = (jnp.arange(slot_count, dtype=jnp.int32)[None, :] < obs_count[0][:, None]).astype(
+    live_mask = (jnp.arange(slot_count, dtype=jnp.int32)[None, :] < counts_here[:, None]).astype(
         jnp.float32
     )
     obs_diff = predicted - target[None]
@@ -53,8 +53,7 @@
         2.0 * members_all * (members_all - 1)
     )
     loss_part = jnp.sum(per_obs * live_mask[None, :, :, None])
-    live_count = jnp.sum(live_mask)
-    live_total = lax.psum(live_count, "grid")
+    live_total = jnp.sum(counts).astype(jnp.float32)
     loss_total = lax.psum(loss_part, ("member", "grid"))
     loss_value = loss_total / (channels * live_total)
     grad_scale = peer_count * peer_count * slot_count / live_total
@@ -76,8 +75,7 @@
     contribution = jnp.einsum(
         "jkp,mjkc->mjpc", norm_weight, grad_interp, preferred_element_type=jnp.float32
     ).astype(jnp.bfloat16)
-    returned = lax.all_to_all(contribution, "grid", split_axis=1, concat_axis=1, tiled=True)
-    summed = jnp.einsum("mdpc,db->mbpc", returned, block_onehot, preferred_element_type=jnp.float32)
+    summed = jnp.einsum("mdpc,db->mbpc", contribution, block_onehot, preferred_element_type=jnp.float32)
     latent_grad = summed.reshape(members_here, points, feature_width)
     return (latent_grad, loss_value)
 

time: 333 us -> 194 us (0.58)
  the two profiles are of different devices: /device:TPU:25 before, /device:TPU:14 now
where the time goes in v1:
time: 194 us; the launch traced here: 193 us
  blocking collectives  89.3 us (46%)
  matrix products  28.1 us (14%)
  local copies, waits for them, and re-layouts  22.2 us (11%)
  between operations  16.6 us (9%)
  other arithmetic  15.9 us (8%)
  starting transfers between devices  13.7 us (7%)
  waiting for transfers between devices  7.32 us (4%)
    all_gather x1, blocking collectives, per_device(): counts = lax.all_gather(obs_count[0], 'grid', axis=0)  46.4 us
    psum x1, blocking collectives, per_device(): loss_total = lax.psum(loss_part, ('member', 'grid'))  43 us
    dot_general x1, matrix products, per_device(): jnp.einsum('rh,ch->rc', grad_act, w_in, preferred_element_type=jnp.float32)  8.8 us
    transpose x1, local copies, waits for them, and re-layouts, per_device(): jnp.einsum('mdpc,db->mbpc', contribution, block_onehot, preferred_element...  8.25 us
    convert_element_type x1, local copies, waits for them, and re-layouts, per_device(): contribution = jnp.einsum('jkp,mjkc->mjpc', norm_weight, grad_interp, pre...  7.97 us
    all_to_all x1, waiting for transfers between devices, per_device(): lax.all_to_all(obs_weight[0], 'grid', split_axis=0, concat_axis=0, tiled=...  7.3 us
    all_to_all x1, starting transfers between devices, per_device(): lax.all_to_all(obs_weight[0], 'grid', split_axis=0, concat_axis=0, tiled=...  7.28 us
    reduce_sum x1, other arithmetic, per_device(): jnp.sum(smooth_abs(pair_diff), axis=1)  7.14 us
  transfers between devices with their start and end apart: 3, of which 1 were waited for; matrix products, arithmetic and copies ran while one was open for 8% of the time, Pallas kernels for 0%

profile of v1, /device:TPU:14, one launch (start us, length us, event | category | flops | bytes accessed | tf_op | source)
XLA Modules:
  0.0 193.2 jit_solution(14607298829665853466)
XLA Ops:
  7.2 0.0 copy-start
  7.2 7.3 %all-to-all-start = ((bf16[16,128,128]{2,1,0:T(8,128)(2,1)}), bf16[16,128,128]{2,1,0:T(8,128)(2,1)S(1)}, u32[]{:S(2)}, u32[]{:S(2)}) async-start(bf16[16,128,128]{2,1,0:T(8,128)(2,1)} %bitcast.68), calls=%async_computation | async-start | bytes 1048576 | tf_op jit(solution)/shard_map/all_to_all | solution.py:31
  14.5 0.0 all-gather.3.cloned.1.call-start
  14.5 0.7 fusion.25
  15.2 5.0 %gather_fusion = bf16[16,2,128,512]{3,2,1,0:T(8,128)(2,1)} fusion(bf16[2,16,128,512]{3,2,1,0:T(8,128)(2,1)} %bitcast.66, s32[1024]{0:T(1024)S(1)} %pad_clamp_fusion), kind=kCustom, calls=%fused_computation | custom fusion | bytes 8388672 | tf_op jit(solution)/shard_map/gather | solution.py:37
  20.2 7.3 %all-to-all-done = bf16[16,128,128]{2,1,0:T(8,128)(2,1)S(1)} async-done(((bf16[16,128,128]{2,1,0:T(8,128)(2,1)}), bf16[16,128,128]{2,1,0:T(8,128)(2,1)S(1)}, u32[]{:S(2)}, u32[]{:S(2)}) %all-to-all-start) | async-done | bytes 524320 | tf_op jit(solution)/shard_map/all_to_all | solution.py:31
  27.5 0.2 convert_reduce_fusion
  27.7 3.5 %convert_bitcast_fusion.1 = bf16[2,16,128,512]{3,2,0,1:T(8,128)(2,1)S(1)} fusion(bf16[16,2,128,512]{3,2,1,0:T(8,128)(2,1)} %gather_fusion, bf16[16,128,128]{2,1,0:T(8,128)(2,1)S(1)} %all-to-all-done, f32[16,128]{1,0:T(8,128)S(1)} %convert_reduce_fusion), kind=kOutput, calls=%fused_computation.17 | convolution fusion | flops 539754496 | bytes 8921088 | tf_op jit(solution)/shard_map/jkp,mjpc->mjkc/dot_general | solution.py:38
  31.2 0.4 copy.17
  31.6 0.0 copy-done
  31.6 0.0 copy-start.6
  31.7 0.0 copy-start.7
  31.7 0.0 copy-start.8
  31.7 2.4 %fusion.28 = f32[4096,512]{1,0:T(8,128)S(1)} fusion(bf16[4096,512]{1,0:T(8,128)(2,1)S(1)} %bitcast.64, bf16[512,512]{1,0:T(8,128)(2,1)S(1)} %copy-done), kind=kOutput, calls=%fused_computation.45 | convolution fusion | flops 2147483648 | bytes 13107200 | tf_op jit(solution)/shard_map/dot_general | solution.py:42
  34.1 0.0 copy-done.6
  34.1 0.0 copy-done.7
  34.1 0.0 copy-done.8
  34.1 0.0 copy-start.3
  34.2 4.1 %convolution_add_fusion = f32[4096,128]{1,0:T(8,128)} fusion(bf16[512,128]{1,0:T(8,128)(2,1)S(1)} %copy-done.6, f32[4096,512]{1,0:T(8,128)S(1)} %fusion.28, f32[512]{0:T(512)S(1)} %copy-done.7, f32[128]{0:T(128)S(1)} %copy-done.8), kind=kOutput, calls=%fused_computation.11 | convolution fusion | flops 549978112 | bytes 10619392 | tf_op jit(solution)/shard_map/dot_general | solution.py:44
  38.2 0.0 copy-done.3
  38.2 0.0 copy-start.5
  38.2 0.0 copy-start.2
  38.2 0.0 all-gather.3.cloned.1.call-update
  38.3 6.4 %all-to-all-start.1 = ((f32[16,128,128]{2,1,0:T(8,128)}), f32[16,128,128]{2,1,0:T(8,128)}, u32[]{:S(2)}, u32[]{:S(2)}) async-start(f32[16,128,128]{2,1,0:T(8,128)} %bitcast.67), calls=%async_computation.1 | async-start | bytes 2097152 | tf_op jit(solution)/shard_map/all_to_all | solution.py:32
  44.7 0.0 copy-done.5
  44.7 46.4 %all-gather = s32[16,1,16]{2,1,0:T(1,128)S(1)} all-gather(s32[1,1,16]{2,1,0:T(1,128)S(1)} %bitcast.72), channel_id=1, replica_groups=mesh['member'=2,'grid'=16] {'grid'}, dimensions={0}, use_global_device_ids=true | all-gather | bytes 1088 | tf_op jit(solution)/shard_map/all_gather | solution.py:33
  91.0 0.4 dynamic-slice_reduce_fusion
  91.5 0.1 fusion.20
  91.6 0.7 reduce_sum.45
  92.9 0.1 fusion.21
  93.0 0.0 all-gather.3.cloned.1.call-done
  93.0 0.0 copy-done.2
  93.0 7.1 %fusion.2 = (f32[2,16,128,128]{3,2,1,0:T(8,128)S(1)}, f32[2,16,128,128]{3,2,1,0:T(8,128)S(1)}) fusion(f32[4,16,128,128]{3,2,1,0:T(8,128)} %all-gather.3.cloned.1.call-done, f32[2,16,128,128]{3,2,1,0:T(8,128)S(1)} %bitcast.63), kind=kLoop, calls=%fused_computation.5 | loop fusion | flops 11534336 | bytes 10485760 | tf_op jit(solution)/shard_map/reduce_sum | solution.py:52
  100.1 2.3 %broadcast_multiply_fusion = (f32[2,16,128,128]{3,2,1,0:T(8,128)}, f32[2,16,128,128]{3,2,1,0:T(8,128)}) fusion(f32[2,16,128,128]{3,2,1,0:T(8,128)S(1)} %get-tuple-element.2, f32[2,16,128,128]{3,2,1,0:T(8,128)S(1)} %get-tuple-element.3), kind=kLoop, calls=%fused_computation.30 | loop fusion | flops 1048576 | bytes 8388608 | tf_op jit(solution)/shard_map/div | solution.py:52
  102.5 0.0 all-to-all-done.1
  102.5 4.8 %fusion.13 = (f32[]{:T(128)}, bf16[4096,128]{1,0:T(8,128)(2,1)}) fusion(f32[2,16,128,128]{3,2,1,0:T(8,128)} %get-tuple-element.6, f32[4096,128]{1,0:T(8,128)S(1)} %copy-done.2, f32[4096]{0:T(1024)S(1)} %bitcast.70, f32[16,128,128]{2,1,0:T(8,128)} %all-to-all-done.1, f32[2,16,128,128]{3,2,1,0:T(8,128)} %get-tuple-element.7, f32[4096]{0:T(1024)S(1)} %bitcast.69), kind=kLoop, calls=%fused_computation.21 | loop fusion | flops 6291455 | bytes 8421380 | tf_op jit(solution)/shard_map/reduce_sum | solution.py:55
  107.3 8.8 %convolution_convert_fusion = bf16[4096,512]{1,0:T(8,128)(2,1)} fusion(bf16[512,512]{1,0:T(8,128)(2,1)S(1)} %copy-done, f32[4096,512]{1,0:T(8,128)} %copy-done.3, bf16[4096,128]{1,0:T(8,128)(2,1)} %get-tuple-element.5, bf16[512,128]{1,0:T(8,128)(2,1)S(1)} %copy-done.6, f32[512]{0:T(512)S(1)} %copy-done.7), kind=kOutput, calls=%fused_computation.10 | convolution fusion | flops 2707423232 | bytes 14288896 | tf_op jit(solution)/shard_map/rh,ch->rc/dot_general | solution.py:71
  116.1 5.9 %convert_bitcast_fusion = bf16[2,16,128,512]{2,3,0,1:T(8,128)(2,1)} fusion(bf16[2,16,128,512]{3,2,1,0:T(8,128)(2,1)} %bitcast.73, bf16[16,128,128]{2,1,0:T(8,128)(2,1)S(1)} %all-to-all-done, f32[16,128]{1,0:T(8,128)S(1)} %convert_reduce_fusion), kind=kOutput, calls=%fused_computation.16 | convolution fusion | flops 539754496 | bytes 8921088 | tf_op jit(solution)/shard_map/jkp,mjkc->mjpc/dot_general | solution.py:75
  121.9 0.0 copy-start.4
  121.9 8.0 %copy.19 = bf16[2,16,128,512]{3,1,2,0:T(8,128)(2,1)} copy(bf16[2,16,128,512]{2,3,0,1:T(8,128)(2,1)} %convert_bitcast_fusion) | data formatting | bytes 8388608 | tf_op jit(solution)/shard_map/convert_element_type | solution.py:77
  129.9 0.0 copy-done.4
  129.9 3.4 %convolution_bitcast_fusion = f32[2,16,128,512]{3,1,2,0:T(8,128)S(1)} fusion(bf16[2,16,128,512]{3,1,2,0:T(8,128)(2,1)} %copy.19, s32[16]{0:T(128)S(1)} %bitcast.71), kind=kOutput, calls=%fused_computation.18 | convolution fusion | flops 67109120 | bytes 12582976 | tf_op jit(solution)/shard_map/mdpc,db->mbpc/dot_general | solution.py:78
  133.3 0.0 copy-start.1
  133.3 8.3 %copy.20 = f32[2,16,128,512]{3,2,1,0:T(8,128)} copy(f32[2,16,128,512]{3,1,2,0:T(8,128)S(1)} %convolution_bitcast_fusion) | data formatting | bytes 16777216 | tf_op jit(solution)/shard_map/mdpc,db->mbpc/transpose | solution.py:78
  141.6 43.0 %psum.7 = f32[]{:T(128)} all-reduce(f32[]{:T(128)} %get-tuple-element.4), channel_id=1, replica_groups=mesh['member'=2,'grid'=16] {'member','grid'}, use_global_device_ids=true, to_apply=%region_5.6 | all-reduce | flops 1 | bytes 8 | tf_op jit(solution)/shard_map/psum | solution.py:57
  185.2 0.0 copy-done.1
  (3 shorter events, 0.0 us)
Async XLA Ops:
  7.2 24.5 %copy-start = (bf16[512,512]{1,0:T(8,128)(2,1)S(1)}, bf16[512,512]{1,0:T(8,128)(2,1)}, u32[]{:S(2)}) copy-start(bf16[512,512]{1,0:T(8,128)(2,1)} %param.14) | copy-start | bytes 1572868
  7.2 20.3 %all-to-all-start = ((bf16[16,128,128]{2,1,0:T(8,128)(2,1)}), bf16[16,128,128]{2,1,0:T(8,128)(2,1)S(1)}, u32[]{:S(2)}, u32[]{:S(2)}) async-start(bf16[16,128,128]{2,1,0:T(8,128)(2,1)} %bitcast.68), calls=%async_computation | async-start | bytes 1048576 | tf_op jit(solution)/shard_map/all_to_all | solution.py:31
  14.5 78.5 %all-gather.3.cloned.1.call-start = ((), (), s32[]{:S(2)}) async-start(), calls=%async_computation.2 | async-start | bytes 6291456 | tf_op jit(solution)/shard_map/all_gather | solution.py:46
  31.6 2.5 %copy-start.6 = (bf16[512,128]{1,0:T(8,128)(2,1)S(1)}, bf16[512,128]{1,0:T(8,128)(2,1)}, u32[]{:S(2)}) copy-start(bf16[512,128]{1,0:T(8,128)(2,1)} %param.16) | copy-start | bytes 393220
  31.7 2.5 %copy-start.7 = (f32[512]{0:T(512)S(1)}, f32[512]{0:T(512)}, u32[]{:S(2)}) copy-start(f32[512]{0:T(512)} %param.15) | copy-start | bytes 6148
  31.7 2.5 %copy-start.8 = (f32[128]{0:T(128)S(1)}, f32[128]{0:T(128)}, u32[]{:S(2)}) copy-start(f32[128]{0:T(128)} %param.17) | copy-start | bytes 1540
  34.1 4.1 %copy-start.3 = (f32[4096,512]{1,0:T(8,128)}, f32[4096,512]{1,0:T(8,128)S(1)}, u32[]{:S(2)}) copy-start(f32[4096,512]{1,0:T(8,128)S(1)} %fusion.28) | copy-start | bytes 25165828
  38.2 6.4 %copy-start.5 = (s32[1,16]{1,0:T(1,128)S(1)}, s32[1,16]{1,0:T(1,128)}, u32[]{:S(2)}) copy-start(s32[1,16]{1,0:T(1,128)} %param.13) | copy-start | bytes 196
  38.2 54.8 %copy-start.2 = (f32[4096,128]{1,0:T(8,128)S(1)}, f32[4096,128]{1,0:T(8,128)}, u32[]{:S(2)}) copy-start(f32[4096,128]{1,0:T(8,128)} %convolution_add_fusion) | copy-start | bytes 6291460
  38.3 64.2 %all-to-all-start.1 = ((f32[16,128,128]{2,1,0:T(8,128)}), f32[16,128,128]{2,1,0:T(8,128)}, u32[]{:S(2)}, u32[]{:S(2)}) async-start(f32[16,128,128]{2,1,0:T(8,128)} %bitcast.67), calls=%async_computation.1 | async-start | bytes 2097152 | tf_op jit(solution)/shard_map/all_to_all | solution.py:32
  121.9 8.0 %copy-start.4 = (s32[1,16]{1,0:T(1,128)S(1)}, s32[1,16]{1,0:T(1,128)}, u32[]{:S(2)}) copy-start(s32[1,16]{1,0:T(1,128)} %param.10) | copy-start | bytes 196
  133.3 51.9 %copy-start.1 = (bf16[512,512]{1,0:T(8,128)(2,1)S(1)}, bf16[512,512]{1,0:T(8,128)(2,1)}, u32[]{:S(2)}) copy-start(bf16[512,512]{1,0:T(8,128)(2,1)} %param.14) | copy-start | bytes 1572868
Sparse Core Ops, SparseCore 0:
  38.4 13.8 all-gather.2

commit v2 on v1

v2 whole, which is shorter than its diff:
```python
import functools

import jax
import jax.numpy as jnp
from jax import lax
from jax.experimental import pallas as pl
from jax.experimental.pallas import tpu as pltpu
from jax.sharding import PartitionSpec as P

SOFTEN = 0.1
F32 = jnp.float32
BF16 = jnp.bfloat16
NT = (((1,), (1,)), ((), ()))


def root_terms(value):
    square = value * value + SOFTEN * SOFTEN
    inverse = lax.rsqrt(square)
    return square * inverse, value * inverse


def network_kernel(
    n, picks, count_in, b_in, w_in, w_out, b_out, w_hbm, o_hbm, lat_hbm,
    contrib_out, loss_out,
    lat, wbuf, obuf, cbuf, wt, slope, preds, peers, gpred, contrib, acc, lbuf,
    sems, lsems, osems,
):
    core = lax.axis_index("member")
    me = lax.axis_index("grid")
    other = 1 - core
    members = lat.shape[0]
    slots, block = wbuf.shape[1] * wbuf.shape[2], wbuf.shape[3]
    channels = obuf.shape[3]
    rows = members * slots
    members_all = 2 * members

    def remote(src, dst, kind, s, target):
        return pltpu.make_async_remote_copy(
            src_ref=src, dst_ref=dst, send_sem=sems.at[kind, s], recv_sem=sems.at[kind + 1, s],
            device_id=target, device_id_type=pl.DeviceIdType.MESH)

    def peer(s):
        return lax.rem(me + s, n)

    def w_copy(s):
        return remote(w_hbm.at[peer(s), core], wbuf.at[s, core], 0, s, (core, peer(s)))

    def o_copy(s):
        return remote(o_hbm.at[peer(s), core], obuf.at[s, core], 2, s, (core, peer(s)))

    def c_copy(s):
        return remote(count_in, cbuf.at[s], 4, s, (core, peer(s)))

    def fw_copy(s, half):
        return remote(wbuf.at[s, half], wbuf.at[s, half], 6, s, (other, me))

    def fo_copy(s, half):
        return remote(obuf.at[s, half], obuf.at[s, half], 8, s, (other, me))

    def p_copy(s):
        return remote(preds.at[s], peers.at[s], 10, s, (other, me))

    def l_copy(s):
        return remote(acc.at[2], lbuf.at[me], 12, s, (core, peer(s)))

    def l_land(s):
        source = lax.rem(me - s + n, n)
        return remote(acc.at[2], lbuf.at[source], 12, s, (core, source))

    lat_copy = pltpu.make_async_copy(lat_hbm, lat, lsems.at[0])
    own_w = pltpu.make_async_copy(w_hbm.at[me], wbuf.at[0], lsems.at[1])
    own_o = pltpu.make_async_copy(o_hbm.at[me], obuf.at[0], lsems.at[2])
    acc_copy = pltpu.make_async_remote_copy(
        src_ref=acc.at[0], dst_ref=acc.at[1], send_sem=lsems.at[3], recv_sem=lsems.at[4],
        device_id=(other, me), device_id_type=pl.DeviceIdType.MESH)
    own_w.start()
    lat_copy.start()
    own_o.start()

    barrier = pltpu.get_barrier_semaphore()
    pl.semaphore_signal(barrier, inc=1, device_id=(other, me), device_id_type=pl.DeviceIdType.MESH)

    @pl.loop(1, n)
    def _(s):
        pl.semaphore_signal(
            barrier, inc=1, device_id=(core, peer(s)), device_id_type=pl.DeviceIdType.MESH)

    pl.semaphore_wait(barrier, n)

    @pl.loop(1, n)
    def _(s):
        c_copy(s).start()

    @pl.loop(1, n)
    def _(s):
        w_copy(s).start()
        o_copy(s).start()

    cbuf[0] = count_in[...]
    acc[0] = jnp.zeros(acc.shape[1:], F32)

    def pass_on(s):
        w_copy(s).wait_recv()
        fw_copy(s, core).start()
        o_copy(s).wait_recv()
        fo_copy(s, core).start()

    def forward(s):
        source = lax.rem(me - s + n, n)
        pick = picks[0, source]
        raw = wbuf[s].reshape(slots, block).astype(F32)
        norm = raw / jnp.sum(raw, axis=1, keepdims=True)
        wt[s] = norm.T.astype(BF16)
        norm = norm.astype(BF16)
        interp = jnp.concatenate([
            jnp.dot(norm, lat[m, pick], preferred_element_type=F32).astype(BF16)
            for m in range(members)], axis=0)
        pre = jnp.dot(interp, w_in[...], preferred_element_type=F32) + b_in[...]
        gate = 0.5 * jnp.tanh(0.5 * pre) + 0.5
        slope[s] = gate * (1.0 + pre * (1.0 - gate))
        hidden = (pre * gate).astype(BF16)
        preds[s] = jnp.dot(hidden, w_out[...], preferred_element_type=F32) + b_out[...]
        p_copy(s).start()

    def counts_total():
        def add(s, total):
            return total + cbuf[s, 0:1, :]
        return jnp.sum(lax.fori_loop(1, n, add, cbuf[0, 0:1, :]), axis=1, keepdims=True)

    def losses(s, scale):
        p_copy(s).wait_recv()
        lane = lax.broadcasted_iota(jnp.int32, (1, cbuf.shape[2]), 1)
        count = jnp.sum(jnp.where(lane == me, cbuf[s, 0:1, :], 0.0), axis=1, keepdims=True)
        slot = lax.broadcasted_iota(jnp.int32, (slots, channels), 0).astype(F32)
        live = slot < count
        target = obuf[s].reshape(slots, channels)
        mine = [preds[s, m * slots:(m + 1) * slots, :] for m in range(members)]
        theirs = [peers[s, m * slots:(m + 1) * slots, :] for m in range(members)]
        near = jnp.zeros((slots, channels), F32)
        pairs = jnp.full((slots, channels), members * SOFTEN, F32)
        slope_obs = []
        slope_pair = [jnp.zeros((slots, channels), F32) for _ in range(members)]
        for i in range(members):
            size, sign = root_terms(mine[i] - target)
            near = near + size
            slope_obs.append(sign)
            for i2 in range(i + 1, members):
                size, sign = root_terms(mine[i] - mine[i2])
                pairs = pairs + 2.0 * size
                slope_pair[i] = slope_pair[i] + sign
                slope_pair[i2] = slope_pair[i2] - sign
            for i2 in range(members):
                size, sign = root_terms(mine[i] - theirs[i2])
                pairs = pairs + size
                slope_pair[i] = slope_pair[i] + sign
        per_obs = near * (1.0 / members_all) - pairs * (1.0 / (2.0 * members_all * (members_all - 1)))
        per_obs = jnp.where(live, per_obs, 0.0)
        acc[0] = acc[0] + jnp.sum(per_obs.reshape(slots // 8, 8, channels), axis=0)
        factor = jnp.where(live, scale, 0.0)
        for i in range(members):
            grad = factor * (slope_obs[i] * (1.0 / members_all)
                             - slope_pair[i] * (1.0 / (members_all * (members_all - 1.0))))
            gpred[s, i * slots:(i + 1) * slots, :] = grad.astype(BF16)

    def backward(s):
        grad_hidden = lax.dot_general(gpred[s], w_out[...], NT, preferred_element_type=F32)
        grad_act = (grad_hidden * slope[s]).astype(BF16)
        grad_interp = lax.dot_general(
            grad_act, w_in[...], NT, preferred_element_type=F32).astype(BF16)
        for m in range(members):
            contrib[s, m] = jnp.dot(
                wt[s], grad_interp[m * slots:(m + 1) * slots, :],
                preferred_element_type=F32).astype(BF16)
        pltpu.make_async_copy(contrib.at[s], contrib_out.at[s], osems.at[s]).start()

    own_w.wait()
    lat_copy.wait()
    own_o.wait()
    forward(0)
    if n > 1:
        pass_on(1)

    @pl.loop(1, n)
    def _(s):
        c_copy(s).wait_recv()

    total = counts_total()
    scale = (n * n * slots) / total

    @pl.loop(1, n)
    def _(s):
        @pl.when(s + 1 < n)
        def _():
            pass_on(s + 1)

        fw_copy(s, other).wait_recv()
        fo_copy(s, other).wait_recv()
        forward(s)
        losses(s - 1, scale)

    losses(n - 1, scale)
    acc_copy.start()
    backward(0)
    acc_copy.wait()
    acc[2] = acc[0] + acc[1]
    lbuf[me] = acc[0] + acc[1]

    @pl.loop(1, n)
    def _(s):
        l_copy(s).start()

    @pl.loop(1, n)
    def _(s):
        backward(s)

    @pl.loop(1, n)
    def _(s):
        l_land(s).wait_recv()

    def add_loss(s, so_far):
        return so_far + lbuf[s]

    loss = lax.fori_loop(1, n, add_loss, lbuf[0])
    loss_out[...] = jnp.broadcast_to(
        jnp.sum(jnp.sum(loss, axis=0, keepdims=True), axis=1, keepdims=True) / (channels * total),
        loss_out.shape)
    p_copy(0).wait_send()

    @pl.loop(1, n)
    def _(s):
        w_copy(s).wait_send()
        o_copy(s).wait_send()
        c_copy(s).wait_send()
        fw_copy(s, core).wait_send()
        fo_copy(s, core).wait_send()
        p_copy(s).wait_send()
        l_copy(s).wait_send()

    @pl.loop(0, n)
    def _(s):
        pltpu.make_async_copy(contrib.at[s], contrib_out.at[s], osems.at[s]).wait()


def scatter_kernel(n, picks, contrib, loss_in, out, loss_out):
    me = lax.axis_index("grid")
    b = pl.program_id(0)
    loss_out[...] = loss_in[...]
    out[...] = jnp.zeros_like(out)

    @pl.loop(0, n)
    def _(s):
        @pl.when(picks[0, lax.rem(me - s + n, n)] == b)
        def _():
            for m in range(out.shape[0]):
                out[m] = out[m] + contrib[s, m].astype(F32)


def per_device(latent, block_pick, obs_weight, obs_value, obs_count, w_in, b_in, w_out, b_out):
    members, points, width = latent.shape
    n = lax.axis_size("grid")
    slots, block = obs_weight.shape[2:]
    channels = obs_value.shape[3]
    inner = w_in.shape[1]
    blocks = points // block
    lanes = -(-n // 128) * 128
    rows = members * slots
    counts = jnp.pad(obs_count.astype(F32), ((0, 7), (0, lanes - n)))
    weights = obs_weight.reshape(n, 2, slots // 2, block)
    values = obs_value.reshape(n, 2, slots // 2, channels)
    vmem = pl.BlockSpec(memory_space=pltpu.VMEM)
    smem = pl.BlockSpec(memory_space=pltpu.SMEM)
    anywhere = pl.BlockSpec(memory_space=pl.ANY)
    contrib, loss = pl.pallas_call(
        functools.partial(network_kernel, n),
        out_shape=(
            jax.ShapeDtypeStruct((n, members, block, width), BF16),
            jax.ShapeDtypeStruct((8, 128), F32),
        ),
        in_specs=[smem] + [vmem] * 5 + [anywhere] * 3,
        out_specs=(anywhere, vmem),
        scratch_shapes=[
            pltpu.VMEM((members, blocks, block, width), BF16),
            pltpu.VMEM((n, 2, slots // 2, block), BF16),
            pltpu.VMEM((n, 2, slots // 2, channels), F32),
            pltpu.VMEM((n, 8, lanes), F32),
            pltpu.VMEM((n, block, slots), BF16),
            pltpu.VMEM((n, rows, inner), F32),
            pltpu.VMEM((n, rows, channels), F32),
            pltpu.VMEM((n, rows, channels), F32),
            pltpu.VMEM((n, rows, channels), BF16),
            pltpu.VMEM((n, members, block, width), BF16),
            pltpu.VMEM((3, 8, channels), F32),
            pltpu.VMEM((n, 8, channels), F32),
            pltpu.SemaphoreType.DMA((14, n)),
            pltpu.SemaphoreType.DMA((5,)),
            pltpu.SemaphoreType.DMA((n,)),
        ],
        compiler_params=pltpu.CompilerParams(
            collective_id=0, has_side_effects=True, vmem_limit_bytes=56 * 1024 * 1024),
        name="network",
    )(block_pick, counts, b_in.reshape(1, -1), w_in, w_out, b_out.reshape(1, -1),
      weights, values, latent.reshape(members, blocks, block, width))
    grad, loss = pl.pallas_call(
        functools.partial(scatter_kernel, n),
        out_shape=(
            jax.ShapeDtypeStruct((members, points, width), F32),
            jax.ShapeDtypeStruct((8, 128), F32),
        ),
        grid=(blocks,),
        in_specs=[smem, pl.BlockSpec((n, members, block, width), lambda b: (0, 0, 0, 0)),
                  pl.BlockSpec((8, 128), lambda b: (0, 0))],
        out_specs=(pl.BlockSpec((members, block, width), lambda b: (0, b, 0)),
                   pl.BlockSpec((8, 128), lambda b: (0, 0))),
        compiler_params=pltpu.CompilerParams(vmem_limit_bytes=32 * 1024 * 1024),
        name="scatter",
    )(block_pick, contrib, loss)
    return (grad, loss[0, 0])


def solution(mesh):
    in_specs = (
        P("member", "grid", None),
        P("grid", None),
        P("grid", None, None, None),
        P("grid", None, None, None),
        P("grid", None),
        P(),
        P(),
        P(),
        P(),
    )
    out_specs = (P("member", "grid", None), P())
    return jax.shard_map(
        per_device, mesh=mesh, in_specs=in_specs, out_specs=out_specs, check_vma=False
    )
```

time: 194 us -> 65.7 us (0.34)
  the two profiles are of different devices: /device:TPU:14 before, /device:TPU:25 now
where the time goes in v2:
time: 65.7 us; the launch traced here: 65.5 us
  Pallas kernels  60.2 us (92%)
  local copies, waits for them, and re-layouts  3.98 us (6%)
  other arithmetic  0.66 us (1%)
  between operations  0.66 us (1%)
    pallas_call x1, Pallas kernels, per_device(): pl.pallas_call(functools.partial(network_kernel, n), out_shape=(jax.Shape...  49.9 us
    pallas_call x1, Pallas kernels, per_device(): pl.pallas_call(functools.partial(scatter_kernel, n), out_shape=(jax.Shape...  10.3 us
    unnamed x6, local copies, waits for them, and re-layouts  2.87 us

profile of v2, /device:TPU:25, one launch (start us, length us, event | category | flops | bytes accessed | tf_op | source)
XLA Modules:
  0.0 65.5 jit_solution(2158152028360927464)
XLA Ops:
  0.6 0.0 copy-start.2
  0.6 0.7 %convert_element_type.5 = f32[1,16]{1,0:T(1,128)S(1)} convert(s32[1,16]{1,0:T(1,128)} %param.13) | non-fusion elementwise | flops 16 | bytes 128 | tf_op jit(solution)/shard_map/convert_element_type | solution.py:267
  1.3 0.6 pad.4.count_in
  1.9 49.9 %network.1 = (bf16[16,2,128,512]{3,2,1,0:T(8,128)(2,1)}, f32[8,128]{1,0:T(8,128)}) custom-call(s32[1,16]{1,0:T(1,128)} %picks.3, f32[8,128]{1,0:T(8,128)} %pad.4.count_in, f32[1,512]{1,0:T(1,128)} %bitcast.9, bf16[512,512]{1,0:T(8,128)(2,1)} %w_in.1, bf16[512,128]{1,0:T(8,128)(2,1)} %w_out.1, f32[1,128]{1,0:T(1,128)} %bitcast.10, ...), custom_call_target="tpu_custom_call" | custom-call | tf_op jit(solution)/shard_map/network/pallas_call | solution.py:273
  51.8 0.0 copy-done.2
  51.8 0.0 copy-start
  51.8 2.2 %copy-done = bf16[16,2,128,512]{3,2,1,0:T(8,128)(2,1)S(1)} copy-done((bf16[16,2,128,512]{3,2,1,0:T(8,128)(2,1)S(1)}, bf16[16,2,128,512]{3,2,1,0:T(8,128)(2,1)}, u32[]{:S(2)}) %copy-start) | copy-done | bytes 4194328
  54.0 0.0 copy-start.1
  54.0 0.7 %copy-done.1 = f32[8,128]{1,0:T(8,128)S(1)} copy-done((f32[8,128]{1,0:T(8,128)S(1)}, f32[8,128]{1,0:T(8,128)}, u32[]{:S(2)}) %copy-start.1) | copy-done | bytes 4120
  54.7 10.3 %scatter.1 = (f32[2,2048,512]{2,1,0:T(8,128)}, f32[8,128]{1,0:T(8,128)S(1)}) custom-call(s32[1,16]{1,0:T(1,128)S(1)} %copy-done.2, bf16[16,2,128,512]{3,2,1,0:T(8,128)(2,1)S(1)} %copy-done, f32[8,128]{1,0:T(8,128)S(1)} %copy-done.1), custom_call_target="tpu_custom_call" | custom-call | tf_op jit(solution)/shard_map/scatter/pallas_call | solution.py:303
  65.0 0.5 slice.3
Async XLA Ops:
  0.6 51.2 %copy-start.2 = (s32[1,16]{1,0:T(1,128)S(1)}, s32[1,16]{1,0:T(1,128)}, u32[]{:S(2)}) copy-start(s32[1,16]{1,0:T(1,128)} %picks.3) | copy-start | bytes 196
  51.8 2.2 %copy-start = (bf16[16,2,128,512]{3,2,1,0:T(8,128)(2,1)S(1)}, bf16[16,2,128,512]{3,2,1,0:T(8,128)(2,1)}, u32[]{:S(2)}) copy-start(bf16[16,2,128,512]{3,2,1,0:T(8,128)(2,1)} %get-tuple-element.6.contrib) | copy-start | bytes 12582916
  54.0 0.7 %copy-start.1 = (f32[8,128]{1,0:T(8,128)S(1)}, f32[8,128]{1,0:T(8,128)}, u32[]{:S(2)}) copy-start(f32[8,128]{1,0:T(8,128)} %get-tuple-element.7.loss_in) | copy-start | bytes 12292

commit v3 on v2

--- a/solution.py
+++ b/solution.py
@@ -8,6 +8,7 @@
 from jax.sharding import PartitionSpec as P
 
 SOFTEN = 0.1
+LOSS_LAG = 2
 F32 = jnp.float32
 BF16 = jnp.bfloat16
 NT = (((1,), (1,)), ((), ()))
@@ -42,6 +43,9 @@
     def peer(s):
         return lax.rem(me + s, n)
 
+    def source_of(s):
+        return lax.rem(me - s + n, n)
+
     def w_copy(s):
         return remote(w_hbm.at[peer(s), core], wbuf.at[s, core], 0, s, (core, peer(s)))
 
@@ -64,7 +68,7 @@
         return remote(acc.at[2], lbuf.at[me], 12, s, (core, peer(s)))
 
     def l_land(s):
-        source = lax.rem(me - s + n, n)
+        source = source_of(s)
         return remote(acc.at[2], lbuf.at[source], 12, s, (core, source))
 
     lat_copy = pltpu.make_async_copy(lat_hbm, lat, lsems.at[0])
@@ -106,8 +110,7 @@
         fo_copy(s, core).start()
 
     def forward(s):
-        source = lax.rem(me - s + n, n)
-        pick = picks[0, source]
+        pick = picks[0, source_of(s)]
         raw = wbuf[s].reshape(slots, block).astype(F32)
         norm = raw / jnp.sum(raw, axis=1, keepdims=True)
         wt[s] = norm.T.astype(BF16)
@@ -120,17 +123,17 @@
         slope[s] = gate * (1.0 + pre * (1.0 - gate))
         hidden = (pre * gate).astype(BF16)
         preds[s] = jnp.dot(hidden, w_out[...], preferred_element_type=F32) + b_out[...]
-        p_copy(s).start()
 
     def counts_total():
         def add(s, total):
-            return total + cbuf[s, 0:1, :]
-        return jnp.sum(lax.fori_loop(1, n, add, cbuf[0, 0:1, :]), axis=1, keepdims=True)
+            return total + cbuf[s]
+        counts = lax.fori_loop(1, n, add, cbuf[0])
+        return jnp.sum(counts.astype(F32), axis=1, keepdims=True)
 
     def losses(s, scale):
-        p_copy(s).wait_recv()
         lane = lax.broadcasted_iota(jnp.int32, (1, cbuf.shape[2]), 1)
-        count = jnp.sum(jnp.where(lane == me, cbuf[s, 0:1, :], 0.0), axis=1, keepdims=True)
+        count = jnp.sum(
+            jnp.where(lane == me, cbuf[s].astype(F32), 0.0), axis=1, keepdims=True)
         slot = lax.broadcasted_iota(jnp.int32, (slots, channels), 0).astype(F32)
         live = slot < count
         target = obuf[s].reshape(slots, channels)
@@ -171,12 +174,16 @@
             contrib[s, m] = jnp.dot(
                 wt[s], grad_interp[m * slots:(m + 1) * slots, :],
                 preferred_element_type=F32).astype(BF16)
+
+    def give(s):
         pltpu.make_async_copy(contrib.at[s], contrib_out.at[s], osems.at[s]).start()
 
     own_w.wait()
     lat_copy.wait()
     own_o.wait()
+    wait = min(LOSS_LAG, n - 1)
     forward(0)
+    p_copy(0).start()
     if n > 1:
         pass_on(1)
 
@@ -187,20 +194,41 @@
     total = counts_total()
     scale = (n * n * slots) / total
 
-    @pl.loop(1, n)
-    def _(s):
+    def ready(s):
         @pl.when(s + 1 < n)
         def _():
             pass_on(s + 1)
 
         fw_copy(s, other).wait_recv()
         fo_copy(s, other).wait_recv()
+
+    @pl.loop(1, wait)
+    def _(s):
+        ready(s)
         forward(s)
-        losses(s - 1, scale)
-
-    losses(n - 1, scale)
+        p_copy(s).start()
+
+    @pl.loop(wait, n)
+    def _(s):
+        ready(s)
+        p_copy(s - wait).wait_recv()
+        losses(s - wait, scale)
+        forward(s)
+        p_copy(s).start()
+
+    @pl.loop(n - wait, n)
+    def _(s):
+        p_copy(s).wait_recv()
+        losses(s, scale)
+
     acc_copy.start()
-    backward(0)
+    middle = min(2, n)
+
+    @pl.loop(0, middle)
+    def _(s):
+        backward(s)
+        give(s)
+
     acc_copy.wait()
     acc[2] = acc[0] + acc[1]
     lbuf[me] = acc[0] + acc[1]
@@ -209,9 +237,10 @@
     def _(s):
         l_copy(s).start()
 
-    @pl.loop(1, n)
+    @pl.loop(middle, n)
     def _(s):
         backward(s)
+        give(s)
 
     @pl.loop(1, n)
     def _(s):
@@ -221,9 +250,8 @@
         return so_far + lbuf[s]
 
     loss = lax.fori_loop(1, n, add_loss, lbuf[0])
-    loss_out[...] = jnp.broadcast_to(
-        jnp.sum(jnp.sum(loss, axis=0, keepdims=True), axis=1, keepdims=True) / (channels * total),
-        loss_out.shape)
+    loss = jnp.sum(loss / (channels * total))
+    loss_out[0, 0] = loss
     p_copy(0).wait_send()
 
     @pl.loop(1, n)
@@ -243,16 +271,21 @@
 
 def scatter_kernel(n, picks, contrib, loss_in, out, loss_out):
     me = lax.axis_index("grid")
-    b = pl.program_id(0)
-    loss_out[...] = loss_in[...]
+    members, block = contrib.shape[1:3]
+    here = out.shape[1] // block
+    first = pl.program_id(0) * here
+    loss_out[0, 0] = loss_in[0, 0]
     out[...] = jnp.zeros_like(out)
 
     @pl.loop(0, n)
     def _(s):
-        @pl.when(picks[0, lax.rem(me - s + n, n)] == b)
+        place = picks[0, lax.rem(me - s + n, n)] - first
+
+        @pl.when((place >= 0) & (place < here))
         def _():
-            for m in range(out.shape[0]):
-                out[m] = out[m] + contrib[s, m].astype(F32)
+            rows = pl.ds(pl.multiple_of(place * block, block), block)
+            for m in range(members):
+                out[m, rows, :] = out[m, rows, :] + contrib[s, m].astype(F32)
 
 
 def per_device(latent, block_pick, obs_weight, obs_value, obs_count, w_in, b_in, w_out, b_out):
@@ -262,9 +295,7 @@
     channels = obs_value.shape[3]
     inner = w_in.shape[1]
     blocks = points // block
-    lanes = -(-n // 128) * 128
     rows = members * slots
-    counts = jnp.pad(obs_count.astype(F32), ((0, 7), (0, lanes - n)))
     weights = obs_weight.reshape(n, 2, slots // 2, block)
     values = obs_value.reshape(n, 2, slots // 2, channels)
     vmem = pl.BlockSpec(memory_space=pltpu.VMEM)
@@ -274,15 +305,15 @@
         functools.partial(network_kernel, n),
         out_shape=(
             jax.ShapeDtypeStruct((n, members, block, width), BF16),
-            jax.ShapeDtypeStruct((8, 128), F32),
+            jax.ShapeDtypeStruct((1, 1), F32),
         ),
         in_specs=[smem] + [vmem] * 5 + [anywhere] * 3,
-        out_specs=(anywhere, vmem),
+        out_specs=(anywhere, smem),
         scratch_shapes=[
             pltpu.VMEM((members, blocks, block, width), BF16),
             pltpu.VMEM((n, 2, slots // 2, block), BF16),
             pltpu.VMEM((n, 2, slots // 2, channels), F32),
-            pltpu.VMEM((n, 8, lanes), F32),
+            pltpu.VMEM((n, 1, n), jnp.int32),
             pltpu.VMEM((n, block, slots), BF16),
             pltpu.VMEM((n, rows, inner), F32),
             pltpu.VMEM((n, rows, channels), F32),
@@ -298,23 +329,23 @@
         compiler_params=pltpu.CompilerParams(
             collective_id=0, has_side_effects=True, vmem_limit_bytes=56 * 1024 * 1024),
         name="network",
-    )(block_pick, counts, b_in.reshape(1, -1), w_in, w_out, b_out.reshape(1, -1),
+    )(block_pick, obs_count, b_in.reshape(1, -1), w_in, w_out, b_out.reshape(1, -1),
       weights, values, latent.reshape(members, blocks, block, width))
+    steps = 4 if blocks % 4 == 0 else 1
     grad, loss = pl.pallas_call(
         functools.partial(scatter_kernel, n),
         out_shape=(
             jax.ShapeDtypeStruct((members, points, width), F32),
-            jax.ShapeDtypeStruct((8, 128), F32),
+            jax.ShapeDtypeStruct((1, 1), F32),
         ),
-        grid=(blocks,),
+        grid=(steps,),
         in_specs=[smem, pl.BlockSpec((n, members, block, width), lambda b: (0, 0, 0, 0)),
-                  pl.BlockSpec((8, 128), lambda b: (0, 0))],
-        out_specs=(pl.BlockSpec((members, block, width), lambda b: (0, b, 0)),
-                   pl.BlockSpec((8, 128), lambda b: (0, 0))),
+                  smem],
+        out_specs=(pl.BlockSpec((members, points // steps, width), lambda b: (0, b, 0)), smem),
         compiler_params=pltpu.CompilerParams(vmem_limit_bytes=32 * 1024 * 1024),
         name="scatter",
     )(block_pick, contrib, loss)
-    return (grad, loss[0, 0])
+    return (grad, loss.reshape(()))
 
 
 def solution(mesh):

time: 65.7 us -> 57.3 us (0.87)
  Pallas kernels: 60.2 us -> 54.3 us
  local copies, waits for them, and re-layouts: 3.98 us -> 2.19 us
  other arithmetic: 0.66 us -> 0 us
    pallas_call x1, Pallas kernels: 10.3 us -> 5.74 us  [per_device(): pl.pallas_call(functools.partial(scatter_kernel, n), out_shape=(jax.Shape...]
    pallas_call x1, Pallas kernels: 49.9 us -> 48.5 us  [per_device(): pl.pallas_call(functools.partial(network_kernel, n), out_shape=(jax.Shape...]
    unnamed x6 -> x4, local copies, waits for them, and re-layouts: 2.87 us -> 2.19 us
    convert_element_type x1 -> x0, other arithmetic: 0.66 us -> none  [per_device(): counts = jnp.pad(obs_count.astype(F32), ((0, 7), (0, lanes - n)))]
where the time goes in v3:
time: 57.3 us; the launch traced here: 57.1 us
  Pallas kernels  54.3 us (95%)
  local copies, waits for them, and re-layouts  2.19 us (4%)
  between operations  0.67 us (1%)
    pallas_call x1, Pallas kernels, per_device(): pl.pallas_call(functools.partial(network_kernel, n), out_shape=(jax.Shape...  48.5 us
    pallas_call x1, Pallas kernels, per_device(): pl.pallas_call(functools.partial(scatter_kernel, n), out_shape=(jax.Shape...  5.74 us
    unnamed x4, local copies, waits for them, and re-layouts  2.19 us

profile of v3, /device:TPU:25, one launch (start us, length us, event | category | flops | bytes accessed | tf_op | source)
XLA Modules:
  0.0 57.1 jit_solution(9083263527608775804)
XLA Ops:
  0.6 0.0 copy-start.1
  0.6 48.5 %network.1 = (bf16[16,2,128,512]{3,2,1,0:T(8,128)(2,1)}, f32[1,1]{1,0:T(1,128)}) custom-call(s32[1,16]{1,0:T(1,128)} %picks.3, s32[1,16]{1,0:T(1,128)} %count_in.1, f32[1,512]{1,0:T(1,128)} %bitcast.9, bf16[512,512]{1,0:T(8,128)(2,1)} %w_in.1, bf16[512,128]{1,0:T(8,128)(2,1)} %w_out.1, f32[1,128]{1,0:T(1,128)} %bitcast.10, bf16[16,2,64,128]{3,2,1,0:T(8,128)(2,1)} %bitcast.8, ...), custom_call_target="tpu_custom_call" | custom-call | tf_op jit(solution)/shard_map/network/pallas_call | solution.py:304
  49.2 0.0 copy-done.1
  49.2 0.0 copy-start
  49.2 2.2 %copy-done = bf16[16,2,128,512]{3,2,1,0:T(8,128)(2,1)S(1)} copy-done((bf16[16,2,128,512]{3,2,1,0:T(8,128)(2,1)S(1)}, bf16[16,2,128,512]{3,2,1,0:T(8,128)(2,1)}, u32[]{:S(2)}) %copy-start) | copy-done | bytes 4194328
  51.4 5.7 %scatter.1 = (f32[2,2048,512]{2,1,0:T(8,128)}, f32[1,1]{1,0:T(1,128)}) custom-call(s32[1,16]{1,0:T(1,128)S(1)} %copy-done.1, bf16[16,2,128,512]{3,2,1,0:T(8,128)(2,1)S(1)} %copy-done, f32[1,1]{1,0:T(1,128)} %get-tuple-element.7.loss_in), custom_call_target="tpu_custom_call" | custom-call | tf_op jit(solution)/shard_map/scatter/pallas_call | solution.py:335
Async XLA Ops:
  0.6 48.6 %copy-start.1 = (s32[1,16]{1,0:T(1,128)S(1)}, s32[1,16]{1,0:T(1,128)}, u32[]{:S(2)}) copy-start(s32[1,16]{1,0:T(1,128)} %picks.3) | copy-start | bytes 196
  49.2 2.2 %copy-start = (bf16[16,2,128,512]{3,2,1,0:T(8,128)(2,1)S(1)}, bf16[16,2,128,512]{3,2,1,0:T(8,128)(2,1)}, u32[]{:S(2)}) copy-start(bf16[16,2,128,512]{3,2,1,0:T(8,128)(2,1)} %get-tuple-element.6.contrib) | copy-start | bytes 12582916
